TPU v7x, 32 devices: a whole 2x2x4 slice. The times are simulated.
32 devices in a mesh: rows: 32 (over z, y, x, core).
Axes of the slice: x: 2, y: 2, z: 4, core: 2. Of those that a mesh axis runs over, the one named last changes fastest.
Arguments:
- snapshots: float32 [262144, 128], P('rows')
- send_list: int32 [1024, 64], P('rows'), may hold values from 0 to 8191
- stencil: int32 [524288, 8], P('rows'), may hold values from 0 to 2047, as said below
- weights: float32 [524288, 8], P('rows'), may hold values from 0.2 to 1
Outputs:
- basis: float32 [524288, 128], P('rows')
- r_factor: float32 [128, 128], replicated
Inputs may be any that keep to these rules, and one draw needn't show every extreme that they name: `send_list`: every slot carries a node; a node may fill several slots. `stencil`: all 8 donors of a row lie on one peer: local row k of device d takes them from peer (d + k // 512) mod 32. Every slot that a device receives is read by some of its rows.
All inputs are finite; a program needn't handle non-finite values.
Results may differ from a plain program's by a relative error of at most 0.0003.
Values sent between devices are 32-bit elements; how exact they have to be, the bound alone decides.
No kernel may reach another device: no remote copies, remote signals or barrier semaphores. Data moves between devices by JAX's collectives and lax.ppermute only.
A program may use at most 192 MiB of HBM per device.

v0:
```python
import jax
import jax.numpy as jnp
from jax import lax
from jax.sharding import PartitionSpec as P


def product(left, right):
    return jnp.dot(left, right, precision=lax.Precision.HIGHEST, preferred_element_type=jnp.float32)


def upper_inverse(upper):
    count = upper.shape[0]
    if count == 1:
        return 1.0 / upper
    half = count // 2
    top_inv = upper_inverse(upper[:half, :half])
    low_inv = upper_inverse(upper[half:, half:])
    corner = -product(product(top_inv, upper[:half, half:]), low_inv)
    zeros_block = jnp.zeros((count - half, half), jnp.float32)
    top_rows = jnp.concatenate([top_inv, corner], axis=1)
    low_rows = jnp.concatenate([zeros_block, low_inv], axis=1)
    return jnp.concatenate([top_rows, low_rows], axis=0)


def normed_factor(block, total_rows):
    local = product(block.T, block)
    gram = lax.psum(local, "rows")
    upper = jnp.linalg.cholesky(gram / total_rows).T
    return upper


def body(snapshots, send_list, stencil, weights):
    peers = lax.axis_size("rows")
    row_count = stencil.shape[0]
    total_rows = row_count * peers
    outgoing = snapshots[send_list]
    received = lax.all_to_all(outgoing, "rows", split_axis=0, concat_axis=0, tiled=True)
    flat = received.reshape(received.shape[0] * received.shape[1], received.shape[2])
    field = jnp.zeros((row_count, flat.shape[1]), jnp.float32)
    for s in range(stencil.shape[1]):
        field = field + weights[:, s][:, None] * flat[stencil[:, s]]
    first = normed_factor(field, total_rows)
    middle = product(field, upper_inverse(first))
    second = normed_factor(middle, total_rows)
    basis = product(middle, upper_inverse(second))
    r_factor = product(second, first)
    return (basis, r_factor)


def solution(mesh):
    return jax.shard_map(
        body,
        mesh=mesh,
        in_specs=(P("rows", None), P("rows", None), P("rows", None), P("rows", None)),
        out_specs=(P("rows", None), P()),
        check_vma=False,
    )
```

profile of v0, /device:TPU:1, one launch (start us, length us, event | category | flops | bytes accessed | tf_op | source)
XLA Modules:
  0.0 1185.2 jit_solution(2221506955138115921)
XLA Ops:
  7.2 0.8 compare_select_fusion.8
  8.1 9.8 gather_fusion
  17.9 7.1 all-to-all-start
  25.9 1.1 fusion.1773
  27.0 23.3 %all-to-all-done = f32[32,64,128]{2,1,0:T(8,128)S(1)} async-done(((f32[32,64,128]{2,1,0:T(8,128)}), f32[32,64,128]{2,1,0:T(8,128)S(1)}, u32[]{:S(2)}, u32[]{:S(2)}) %all-to-all-start) | async-done | bytes 1048608 | tf_op jit(solution)/shard_map/all_to_all | solution.py:37
  50.3 54.7 %gather_fusion.1 = f32[16384,128]{1,0:T(8,128)} fusion(f32[2048,128]{1,0:T(8,128)S(1)} %bitcast.288, s32[16384]{0:T(1024)S(1)} %broadcast_clamp_fusion.7), kind=kCustom, calls=%fused_computation.1 | custom fusion | bytes 16842752 | tf_op jit(solution)/shard_map/gather | solution.py:41
  105.1 54.8 %gather_fusion.2 = f32[16384,128]{1,0:T(8,128)} fusion(f32[2048,128]{1,0:T(8,128)S(1)} %bitcast.289, s32[16384]{0:T(1024)S(1)} %broadcast_clamp_fusion.6), kind=kCustom, calls=%fused_computation.2 | custom fusion | bytes 16842752 | tf_op jit(solution)/shard_map/gather | solution.py:41
  159.9 54.8 %gather_fusion.3 = f32[16384,128]{1,0:T(8,128)} fusion(f32[2048,128]{1,0:T(8,128)S(1)} %bitcast.290, s32[16384]{0:T(1024)S(1)} %broadcast_clamp_fusion.5), kind=kCustom, calls=%fused_computation.3 | custom fusion | bytes 16842752 | tf_op jit(solution)/shard_map/gather | solution.py:41
  214.6 54.8 %gather_fusion.4 = f32[16384,128]{1,0:T(8,128)} fusion(f32[2048,128]{1,0:T(8,128)S(1)} %bitcast.291, s32[16384]{0:T(1024)S(1)} %broadcast_clamp_fusion.4), kind=kCustom, calls=%fused_computation.4 | custom fusion | bytes 16842752 | tf_op jit(solution)/shard_map/gather | solution.py:41
  269.4 54.8 %gather_fusion.5 = f32[16384,128]{1,0:T(8,128)} fusion(f32[2048,128]{1,0:T(8,128)S(1)} %bitcast.292, s32[16384]{0:T(1024)S(1)} %broadcast_clamp_fusion.3), kind=kCustom, calls=%fused_computation.5 | custom fusion | bytes 16842752 | tf_op jit(solution)/shard_map/gather | solution.py:41
  324.2 54.8 %gather_fusion.6 = f32[16384,128]{1,0:T(8,128)} fusion(f32[2048,128]{1,0:T(8,128)S(1)} %bitcast.293, s32[16384]{0:T(1024)S(1)} %broadcast_clamp_fusion.2), kind=kCustom, calls=%fused_computation.6 | custom fusion | bytes 16842752 | tf_op jit(solution)/shard_map/gather | solution.py:41
  379.0 54.7 %gather_fusion.7 = f32[16384,128]{1,0:T(8,128)} fusion(f32[2048,128]{1,0:T(8,128)S(1)} %bitcast.294, s32[16384]{0:T(1024)S(1)} %broadcast_clamp_fusion.1), kind=kCustom, calls=%fused_computation.7 | custom fusion | bytes 16842752 | tf_op jit(solution)/shard_map/gather | solution.py:41
  433.8 54.9 %gather_fusion.8 = f32[16384,128]{1,0:T(8,128)} fusion(f32[2048,128]{1,0:T(8,128)S(1)} %bitcast.295, s32[16384]{0:T(1024)S(1)} %broadcast_clamp_fusion), kind=kCustom, calls=%fused_computation.8 | custom fusion | bytes 16842752 | tf_op jit(solution)/shard_map/gather | solution.py:41
  488.7 25.8 %multiply_add_fusion = f32[16384,128]{1,0:T(8,128)S(1)} fusion(f32[16384,128]{1,0:T(8,128)} %gather_fusion.8, f32[16384,128]{1,0:T(8,128)} %gather_fusion.7, f32[16384,128]{1,0:T(8,128)} %gather_fusion.6, f32[16384,128]{1,0:T(8,128)} %gather_fusion.5, f32[16384,128]{1,0:T(8,128)} %gather_fusion.4, f32[16384,128]{1,0:T(8,128)} %gather_fusion.3, ...), kind=kLoop, calls=%fused_computation.9 | loop fusion | flops 31457280 | bytes 76021760 | tf_op jit(solution)/shard_map/add | solution.py:41
  514.5 3.4 copy-done.1
  517.9 14.9 %fusion.1794 = f32[128,128]{0,1:T(8,128)} fusion(f32[16384,128]{1,0:T(8,128)S(1)} %multiply_add_fusion), kind=kOutput, calls=%fused_computation.2092 | convolution fusion | flops 3221225472 | bytes 8454144 | tf_op jit(solution)/shard_map/dot_general | solution.py:8
  532.8 118.9 %all-reduce.129.cloned.1.call-done = f32[128,128]{0,1:T(8,128)} async-done(((f32[128,128]{0,1:T(8,128)}), f32[128,128]{0,1:T(8,128)}) %all-reduce.129.cloned.1.call-update) | async-done | bytes 65552 | tf_op jit(solution)/shard_map/psum | solution.py:27
  651.7 0.8 broadcast_multiply_fusion.1
  652.7 0.9 fusion.65
  653.5 11.7 cholesky.44
  666.5 0.7 fusion.1785
  667.2 0.7 fusion.1784
  668.6 0.7 fusion.1787
  669.4 0.7 fusion.1788
  670.7 0.7 fusion.1790
  671.4 0.7 fusion.1789
  672.1 0.7 fusion.1791
  672.9 0.7 fusion.1792
  673.6 0.7 fusion.1793
  831.1 10.1 fusion.13
  841.2 3.3 copy-done
  844.5 14.6 %fusion.1795 = f32[128,128]{0,1:T(8,128)} fusion(f32[16384,128]{1,0:T(8,128)S(1)} %fusion.13), kind=kOutput, calls=%fused_computation.2093 | convolution fusion | flops 3221225472 | bytes 8454144 | tf_op jit(solution)/shard_map/dot_general | solution.py:8
  859.1 118.5 %all-reduce.131.cloned.1.call-done = f32[128,128]{0,1:T(8,128)} async-done(((f32[128,128]{0,1:T(8,128)}), f32[128,128]{0,1:T(8,128)}) %all-reduce.131.cloned.1.call-update) | async-done | bytes 65552 | tf_op jit(solution)/shard_map/psum | solution.py:27
  977.6 0.8 broadcast_multiply_fusion
  978.5 0.9 fusion.64
  979.4 11.7 cholesky.55
  991.8 2.1 fusion.66
  994.6 0.7 fusion.1775
  995.3 0.7 fusion.1774
  996.0 0.7 fusion.1776
  996.8 0.7 fusion.1778
  997.5 0.7 fusion.1777
  998.8 0.7 fusion.1780
  999.6 0.7 fusion.1779
  1000.3 0.7 fusion.1781
  1001.0 0.7 fusion.1783
  1001.8 0.7 fusion.1782
  1160.7 17.2 %fusion.28 = f32[16384,128]{1,0:T(8,128)} fusion(f32[16384,128]{1,0:T(8,128)} %copy-done, f32[1,1]{0,1:T(1,128)} %constant.46.clone.1, f32[64,64]{0,1:T(8,128)S(1)} %fusion.116, f32[64,64]{0,1:T(8,128)S(1)} %convolution_negate_fusion, f32[32,64]{0,1:T(8,128)S(1)} %concatenate.2854, f32[32,32]{0,1:T(8,128)S(1)} %convolution_negate_fusion.3, ...), kind=kOutput, calls=%fused_computation.185 | convolution fusion | flops 3221504000 | bytes 16826368 | tf_op jit(solution)/shard_map/dot_general | solution.py:8
  (478 shorter events, 68.8 us)
Async XLA Ops:
  7.2 17.9 %copy-start.2 = (s32[16384,8]{0,1:T(8,128)S(1)}, s32[16384,8]{0,1:T(8,128)}, u32[]{:S(2)}) copy-start(s32[16384,8]{0,1:T(8,128)} %param.7) | copy-start | bytes 1572868
  7.2 18.7 %copy-start.3 = (f32[16384,8]{0,1:T(8,128)S(1)}, f32[16384,8]{0,1:T(8,128)}, u32[]{:S(2)}) copy-start(f32[16384,8]{0,1:T(8,128)} %param.8) | copy-start | bytes 1572868
  17.9 32.4 %all-to-all-start = ((f32[32,64,128]{2,1,0:T(8,128)}), f32[32,64,128]{2,1,0:T(8,128)S(1)}, u32[]{:S(2)}, u32[]{:S(2)}) async-start(f32[32,64,128]{2,1,0:T(8,128)} %bitcast.1), calls=%async_computation | async-start | bytes 2097152 | tf_op jit(solution)/shard_map/all_to_all | solution.py:37
  25.0 626.7 %all-reduce.129.cloned.1.call-start = ((), (), s32[]{:S(2)}) async-start(), calls=%async_computation.1 | async-start | bytes 131072 | tf_op jit(solution)/shard_map/psum | solution.py:27
  433.7 54.9 %copy-start.4 = (f32[16384,1]{0,1:T(1,128)S(1)}, f32[16384,1]{0,1:T(1,128)}, u32[]{:S(2)}) copy-start(f32[16384,1]{0,1:T(1,128)} %get-tuple-element.3) | copy-start | bytes 196612
  433.7 54.9 %copy-start.5 = (f32[16384,1]{0,1:T(1,128)S(1)}, f32[16384,1]{0,1:T(1,128)}, u32[]{:S(2)}) copy-start(f32[16384,1]{0,1:T(1,128)} %get-tuple-element.4) | copy-start | bytes 196612
  433.7 54.9 %copy-start.6 = (f32[16384,1]{0,1:T(1,128)S(1)}, f32[16384,1]{0,1:T(1,128)}, u32[]{:S(2)}) copy-start(f32[16384,1]{0,1:T(1,128)} %get-tuple-element.5) | copy-start | bytes 196612
  433.7 54.9 %copy-start.7 = (f32[16384,1]{0,1:T(1,128)S(1)}, f32[16384,1]{0,1:T(1,128)}, u32[]{:S(2)}) copy-start(f32[16384,1]{0,1:T(1,128)} %get-tuple-element.6) | copy-start | bytes 196612
  433.8 54.9 %copy-start.8 = (f32[16384,1]{0,1:T(1,128)S(1)}, f32[16384,1]{0,1:T(1,128)}, u32[]{:S(2)}) copy-start(f32[16384,1]{0,1:T(1,128)} %get-tuple-element.7) | copy-start | bytes 196612
  433.8 54.9 %copy-start.9 = (f32[16384,1]{0,1:T(1,128)S(1)}, f32[16384,1]{0,1:T(1,128)}, u32[]{:S(2)}) copy-start(f32[16384,1]{0,1:T(1,128)} %get-tuple-element.8) | copy-start | bytes 196612
  433.8 54.9 %copy-start.10 = (f32[16384,1]{0,1:T(1,128)S(1)}, f32[16384,1]{0,1:T(1,128)}, u32[]{:S(2)}) copy-start(f32[16384,1]{0,1:T(1,128)} %get-tuple-element.9) | copy-start | bytes 196612
  433.8 54.9 %copy-start.11 = (f32[16384,1]{0,1:T(1,128)S(1)}, f32[16384,1]{0,1:T(1,128)}, u32[]{:S(2)}) copy-start(f32[16384,1]{0,1:T(1,128)} %get-tuple-element.10) | copy-start | bytes 196612
  514.5 3.4 copy-start.1
  532.8 444.8 %all-reduce.131.cloned.1.call-start = ((), (), s32[]{:S(2)}) async-start(), calls=%async_computation.2 | async-start | bytes 131072 | tf_op jit(solution)/shard_map/psum | solution.py:27
  841.2 3.3 copy-start
Sparse Core Ops, SparseCore 0:
  532.9 118.7 all-reduce.128
  859.2 118.3 all-reduce.130
where the time goes:
time: 1190 us
  local copies, waits for them, and re-layouts  474 us (40%)
  between operations  267 us (22%)
  waiting for transfers between devices  261 us (22%)
  matrix products  111 us (9%)
  other arithmetic  66.1 us (6%)
    gather x8, local copies, waits for them, and re-layouts, body(): field = field + weights[:, s][:, None] * flat[stencil[:, s]]  438 us
    psum x2, waiting for transfers between devices, normed_factor(): gram = lax.psum(local, 'rows')  237 us
    dot_general x257, matrix products, product(): jnp.dot(left, right, precision=lax.Precision.HIGHEST, preferred_element_t...  111 us
    add x1, other arithmetic, body(): field = field + weights[:, s][:, None] * flat[stencil[:, s]]  25.8 us
    another operation x6, other arithmetic, normed_factor(): upper = jnp.linalg.cholesky(gram / total_rows).T  24.8 us
  transfers between devices with their start and end apart: 3, of which 3 were waited for; matrix products, arithmetic and copies ran while one was open for 0% of the time, Pallas kernels for 0%

commit v1 on v0

--- a/solution.py
+++ b/solution.py
@@ -24,7 +24,7 @@
 
 def normed_factor(block, total_rows):
     local = product(block.T, block)
-    gram = lax.psum(local, "rows")
+    gram = jnp.sum(lax.all_gather(local, "rows"), axis=0)
     upper = jnp.linalg.cholesky(gram / total_rows).T
     return upper
 

time: 1190 us -> 1070 us (0.90)
  waiting for transfers between devices: 261 us -> 135 us
    psum x2 -> x0, waiting for transfers between devices: 237 us -> none  [normed_factor(): gram = lax.psum(local, 'rows')]
    all_gather x0 -> x2, waiting for transfers between devices: none -> 112 us  [normed_factor(): gram = jnp.sum(lax.all_gather(local, 'rows'), axis=0)]
where the time goes in v1:
time: 1070 us; the launch traced here: 1060 us
  local copies, waits for them, and re-layouts  474 us (44%)
  between operations  267 us (25%)
  waiting for transfers between devices  135 us (13%)
  matrix products  111 us (10%)
  other arithmetic  66.2 us (6%)
    gather x8, local copies, waits for them, and re-layouts, body(): field = field + weights[:, s][:, None] * flat[stencil[:, s]]  438 us
    all_gather x2, waiting for transfers between devices, normed_factor(): gram = jnp.sum(lax.all_gather(local, 'rows'), axis=0)  112 us
    dot_general x257, matrix products, product(): jnp.dot(left, right, precision=lax.Precision.HIGHEST, preferred_element_t...  111 us
    add x1, other arithmetic, body(): field = field + weights[:, s][:, None] * flat[stencil[:, s]]  25.8 us
    another operation x6, other arithmetic, normed_factor(): upper = jnp.linalg.cholesky(gram / total_rows).T  24.8 us
    all_to_all x1, waiting for transfers between devices, body(): lax.all_to_all(outgoing, 'rows', split_axis=0, concat_axis=0, tiled=True)  23.3 us
  transfers between devices with their start and end apart: 3, of which 3 were waited for; matrix products, arithmetic and copies ran while one was open for 0% of the time, Pallas kernels for 0%

profile of v1, /device:TPU:1, one launch (start us, length us, event | category | flops | bytes accessed | tf_op | source)
XLA Modules:
  0.0 1060.0 jit_solution(8566605355683661647)
XLA Ops:
  7.2 0.8 compare_select_fusion.8
  8.1 9.8 gather_fusion
  17.9 7.1 all-to-all-start
  25.1 0.7 compare_select_fusion.7
  25.9 1.1 fusion.1773
  27.0 23.3 %all-to-all-done = f32[32,64,128]{2,1,0:T(8,128)S(1)} async-done(((f32[32,64,128]{2,1,0:T(8,128)}), f32[32,64,128]{2,1,0:T(8,128)S(1)}, u32[]{:S(2)}, u32[]{:S(2)}) %all-to-all-start) | async-done | bytes 1048608 | tf_op jit(solution)/shard_map/all_to_all | solution.py:37
  50.3 54.7 %gather_fusion.1 = f32[16384,128]{1,0:T(8,128)} fusion(f32[2048,128]{1,0:T(8,128)S(1)} %bitcast.290, s32[16384]{0:T(1024)S(1)} %broadcast_clamp_fusion.7), kind=kCustom, calls=%fused_computation.1 | custom fusion | bytes 16842752 | tf_op jit(solution)/shard_map/gather | solution.py:41
  105.1 54.8 %gather_fusion.2 = f32[16384,128]{1,0:T(8,128)} fusion(f32[2048,128]{1,0:T(8,128)S(1)} %bitcast.291, s32[16384]{0:T(1024)S(1)} %broadcast_clamp_fusion.6), kind=kCustom, calls=%fused_computation.2 | custom fusion | bytes 16842752 | tf_op jit(solution)/shard_map/gather | solution.py:41
  159.9 54.8 %gather_fusion.3 = f32[16384,128]{1,0:T(8,128)} fusion(f32[2048,128]{1,0:T(8,128)S(1)} %bitcast.292, s32[16384]{0:T(1024)S(1)} %broadcast_clamp_fusion.5), kind=kCustom, calls=%fused_computation.3 | custom fusion | bytes 16842752 | tf_op jit(solution)/shard_map/gather | solution.py:41
  214.6 54.8 %gather_fusion.4 = f32[16384,128]{1,0:T(8,128)} fusion(f32[2048,128]{1,0:T(8,128)S(1)} %bitcast.293, s32[16384]{0:T(1024)S(1)} %broadcast_clamp_fusion.4), kind=kCustom, calls=%fused_computation.4 | custom fusion | bytes 16842752 | tf_op jit(solution)/shard_map/gather | solution.py:41
  269.4 54.8 %gather_fusion.5 = f32[16384,128]{1,0:T(8,128)} fusion(f32[2048,128]{1,0:T(8,128)S(1)} %bitcast.294, s32[16384]{0:T(1024)S(1)} %broadcast_clamp_fusion.3), kind=kCustom, calls=%fused_computation.5 | custom fusion | bytes 16842752 | tf_op jit(solution)/shard_map/gather | solution.py:41
  324.2 54.8 %gather_fusion.6 = f32[16384,128]{1,0:T(8,128)} fusion(f32[2048,128]{1,0:T(8,128)S(1)} %bitcast.295, s32[16384]{0:T(1024)S(1)} %broadcast_clamp_fusion.2), kind=kCustom, calls=%fused_computation.6 | custom fusion | bytes 16842752 | tf_op jit(solution)/shard_map/gather | solution.py:41
  379.0 54.7 %gather_fusion.7 = f32[16384,128]{1,0:T(8,128)} fusion(f32[2048,128]{1,0:T(8,128)S(1)} %bitcast.296, s32[16384]{0:T(1024)S(1)} %broadcast_clamp_fusion.1), kind=kCustom, calls=%fused_computation.7 | custom fusion | bytes 16842752 | tf_op jit(solution)/shard_map/gather | solution.py:41
  433.8 54.9 %gather_fusion.8 = f32[16384,128]{1,0:T(8,128)} fusion(f32[2048,128]{1,0:T(8,128)S(1)} %bitcast.297, s32[16384]{0:T(1024)S(1)} %broadcast_clamp_fusion), kind=kCustom, calls=%fused_computation.8 | custom fusion | bytes 16842752 | tf_op jit(solution)/shard_map/gather | solution.py:41
  488.7 25.8 %multiply_add_fusion = f32[16384,128]{1,0:T(8,128)S(1)} fusion(f32[16384,128]{1,0:T(8,128)} %gather_fusion.8, f32[16384,128]{1,0:T(8,128)} %gather_fusion.7, f32[16384,128]{1,0:T(8,128)} %gather_fusion.6, f32[16384,128]{1,0:T(8,128)} %gather_fusion.5, f32[16384,128]{1,0:T(8,128)} %gather_fusion.4, f32[16384,128]{1,0:T(8,128)} %gather_fusion.3, ...), kind=kLoop, calls=%fused_computation.9 | loop fusion | flops 31457280 | bytes 76021760 | tf_op jit(solution)/shard_map/add | solution.py:41
  514.5 3.4 copy-done.1
  517.9 14.9 %fusion.1794 = f32[128,128]{1,0:T(8,128)} fusion(f32[16384,128]{1,0:T(8,128)S(1)} %multiply_add_fusion), kind=kOutput, calls=%fused_computation.2092 | convolution fusion | flops 3221225472 | bytes 8454144 | tf_op jit(solution)/shard_map/dot_general | solution.py:8
  532.8 56.4 %all-gather.5.cloned.1.call-done = f32[4096,128]{1,0:T(8,128)} async-done(((f32[128,128]{1,0:T(8,128)}), f32[4096,128]{1,0:T(8,128)}) %all-gather.5.cloned.1.call-update) | async-done | bytes 2097168 | tf_op jit(solution)/shard_map/all_gather | solution.py:27
  589.2 1.7 reduce_sum.18
  591.2 11.7 %cholesky.44 = f32[128,128]{1,0:T(8,128)S(1)} custom-call(f32[128,128]{1,0:T(8,128)S(1)} %fusion.65), custom_call_target="Cholesky" | custom-call | tf_op jit(solution)/shard_map/jit(cholesky)/cholesky | solution.py:28
  604.2 0.7 fusion.1785
  605.0 0.7 fusion.1784
  605.7 0.7 fusion.1786
  606.4 0.7 fusion.1787
  607.1 0.7 fusion.1788
  608.4 0.7 fusion.1790
  609.2 0.7 fusion.1789
  609.9 0.7 fusion.1791
  610.6 0.7 fusion.1792
  611.4 0.7 fusion.1793
  768.9 10.1 fusion.13
  779.0 3.3 copy-done
  782.2 14.6 %fusion.1795 = f32[128,128]{1,0:T(8,128)} fusion(f32[16384,128]{1,0:T(8,128)S(1)} %fusion.13), kind=kOutput, calls=%fused_computation.2093 | convolution fusion | flops 3221225472 | bytes 8454144 | tf_op jit(solution)/shard_map/dot_general | solution.py:8
  796.9 55.4 %all-gather.7.cloned.1.call-done = f32[4096,128]{1,0:T(8,128)} async-done(((f32[128,128]{1,0:T(8,128)}), f32[4096,128]{1,0:T(8,128)}) %all-gather.7.cloned.1.call-update) | async-done | bytes 2097168 | tf_op jit(solution)/shard_map/all_gather | solution.py:27
  852.2 1.7 reduce_sum.19
  854.2 11.7 %cholesky.55 = f32[128,128]{1,0:T(8,128)S(1)} custom-call(f32[128,128]{1,0:T(8,128)S(1)} %fusion.64), custom_call_target="Cholesky" | custom-call | tf_op jit(solution)/shard_map/jit(cholesky)/cholesky | solution.py:28
  866.6 2.2 fusion.66
  869.4 0.7 fusion.1775
  870.2 0.7 fusion.1774
  870.9 0.7 fusion.1776
  871.6 0.7 fusion.1778
  872.4 0.7 fusion.1777
  873.7 0.7 fusion.1780
  874.4 0.7 fusion.1779
  875.2 0.7 fusion.1781
  875.9 0.7 fusion.1783
  876.6 0.7 fusion.1782
  1035.6 17.2 %fusion.28 = f32[16384,128]{1,0:T(8,128)} fusion(f32[16384,128]{1,0:T(8,128)} %copy-done, f32[1,1]{0,1:T(1,128)} %constant.48.clone.1, f32[64,64]{0,1:T(8,128)S(1)} %fusion.116, f32[64,64]{0,1:T(8,128)S(1)} %convolution_negate_fusion, f32[32,64]{0,1:T(8,128)S(1)} %concatenate.2854, f32[32,32]{0,1:T(8,128)S(1)} %convolution_negate_fusion.3, ...), kind=kOutput, calls=%fused_computation.185 | convolution fusion | flops 3221504000 | bytes 16826368 | tf_op jit(solution)/shard_map/dot_general | solution.py:8
  (482 shorter events, 67.7 us)
Async XLA Ops:
  7.2 17.9 %copy-start.2 = (s32[16384,8]{0,1:T(8,128)S(1)}, s32[16384,8]{0,1:T(8,128)}, u32[]{:S(2)}) copy-start(s32[16384,8]{0,1:T(8,128)} %param.7) | copy-start | bytes 1572868
  7.2 18.7 %copy-start.3 = (f32[16384,8]{0,1:T(8,128)S(1)}, f32[16384,8]{0,1:T(8,128)}, u32[]{:S(2)}) copy-start(f32[16384,8]{0,1:T(8,128)} %param.8) | copy-start | bytes 1572868
  17.9 32.4 %all-to-all-start = ((f32[32,64,128]{2,1,0:T(8,128)}), f32[32,64,128]{2,1,0:T(8,128)S(1)}, u32[]{:S(2)}, u32[]{:S(2)}) async-start(f32[32,64,128]{2,1,0:T(8,128)} %bitcast.1), calls=%async_computation | async-start | bytes 2097152 | tf_op jit(solution)/shard_map/all_to_all | solution.py:37
  25.0 564.2 %all-gather.5.cloned.1.call-start = ((), (), s32[]{:S(2)}) async-start(), calls=%async_computation.1 | async-start | bytes 2162688 | tf_op jit(solution)/shard_map/all_gather | solution.py:27
  433.7 54.9 %copy-start.4 = (f32[16384,1]{0,1:T(1,128)S(1)}, f32[16384,1]{0,1:T(1,128)}, u32[]{:S(2)}) copy-start(f32[16384,1]{0,1:T(1,128)} %get-tuple-element.3) | copy-start | bytes 196612
  433.7 54.9 %copy-start.5 = (f32[16384,1]{0,1:T(1,128)S(1)}, f32[16384,1]{0,1:T(1,128)}, u32[]{:S(2)}) copy-start(f32[16384,1]{0,1:T(1,128)} %get-tuple-element.4) | copy-start | bytes 196612
  433.7 54.9 %copy-start.6 = (f32[16384,1]{0,1:T(1,128)S(1)}, f32[16384,1]{0,1:T(1,128)}, u32[]{:S(2)}) copy-start(f32[16384,1]{0,1:T(1,128)} %get-tuple-element.5) | copy-start | bytes 196612
  433.7 54.9 %copy-start.7 = (f32[16384,1]{0,1:T(1,128)S(1)}, f32[16384,1]{0,1:T(1,128)}, u32[]{:S(2)}) copy-start(f32[16384,1]{0,1:T(1,128)} %get-tuple-element.6) | copy-start | bytes 196612
  433.8 54.9 %copy-start.8 = (f32[16384,1]{0,1:T(1,128)S(1)}, f32[16384,1]{0,1:T(1,128)}, u32[]{:S(2)}) copy-start(f32[16384,1]{0,1:T(1,128)} %get-tuple-element.7) | copy-start | bytes 196612
  433.8 54.9 %copy-start.9 = (f32[16384,1]{0,1:T(1,128)S(1)}, f32[16384,1]{0,1:T(1,128)}, u32[]{:S(2)}) copy-start(f32[16384,1]{0,1:T(1,128)} %get-tuple-element.8) | copy-start | bytes 196612
  433.8 54.9 %copy-start.10 = (f32[16384,1]{0,1:T(1,128)S(1)}, f32[16384,1]{0,1:T(1,128)}, u32[]{:S(2)}) copy-start(f32[16384,1]{0,1:T(1,128)} %get-tuple-element.9) | copy-start | bytes 196612
  433.8 54.9 %copy-start.11 = (f32[16384,1]{0,1:T(1,128)S(1)}, f32[16384,1]{0,1:T(1,128)}, u32[]{:S(2)}) copy-start(f32[16384,1]{0,1:T(1,128)} %get-tuple-element.10) | copy-start | bytes 196612
  514.5 3.4 copy-start.1
  532.8 319.5 %all-gather.7.cloned.1.call-start = ((), (), s32[]{:S(2)}) async-start(), calls=%async_computation.2 | async-start | bytes 2162688 | tf_op jit(solution)/shard_map/all_gather | solution.py:27
  779.0 3.3 copy-start
Sparse Core Ops, SparseCore 0:
  532.9 56.2 all-gather.4
  797.0 55.2 all-gather.6
